TPU v7x, 256 devices: a whole 4x4x8 slice. The times are simulated.
256 devices in a mesh: dp: 4 (over x_hi, core), sx: 8 (over y, x_lo), syz: 8 (over z).
Axes of the slice: x: 4 (x_hi: 2, x_lo: 2; x = x_hi * 2 + x_lo), y: 4, z: 8, core: 2. Of those that a mesh axis runs over, the one named last changes fastest.
Arguments:
- input_act: bfloat16 [4, 32, 128, 64, 128], P('dp', 'sx', 'syz'), may hold values from -6 to 6
- pre_act: bfloat16 [4, 16, 64, 64, 128], P('dp', 'sx', 'syz'), may hold values from -6 to 6
- out_grad: bfloat16 [4, 8, 32, 32, 128], P('dp', 'sx', 'syz'), may hold values from -24 to 24
- weight_one: bfloat16 [3, 3, 3, 64, 128], replicated, may hold values from -0.15625 to 0.15625
- weight_two: bfloat16 [3, 3, 3, 128, 128], replicated, may hold values from -0.109375 to 0.109375
Outputs:
- grad_input: bfloat16 [4, 32, 128, 64, 128], P('dp', 'sx', 'syz')
- grad_one: float32 [3, 3, 3, 64, 128], replicated
- grad_two: float32 [3, 3, 3, 128, 128], replicated
All inputs are finite; a program needn't handle non-finite values.
Results may differ from a plain program's by a relative error of at most 0.0049.
Values may be sent and summed in bfloat16 or wider, within the bound.
No kernel may reach another device: no remote copies, remote signals or barrier semaphores. Data moves between devices by JAX's collectives and lax.ppermute only.
A program may use at most 64 MiB of HBM per device.

v0:
```python
import functools

import jax
import jax.numpy as jnp
from jax import lax
from jax.experimental import pallas as pl
from jax.experimental.pallas import tpu as pltpu
from jax.sharding import Mesh
from jax.sharding import PartitionSpec as P


BF = jnp.bfloat16
F32 = jnp.float32

CY, CZ = 4, 32
MX, MY, MZ = 2, 8, 64
CIN, C1, C2 = 64, 128, 128
EX, EY = MX + 1, MY + 1
CHUNK = 88
AX = ("y", "xl")
AZ = ("zh", "zl")
GROUP = 32
HALF = CHUNK * GROUP
ROWS_ONE = 27 * CIN
ROWS_TWO = 27 * C1
SCALE_ONE = float(4 * 16 * 64 * 64) ** (-0.5)
SCALE_TWO = float(4 * 8 * 32 * 32) ** (-0.5)

TAP = ((1, 1), (0, 0), (1, 0))
TAPS = (((1, 0),), ((2, 0), (0, 1)))
SLOT = (2, 0, 1)


def nt(a, b):
    return lax.dot_general(a, b, (((1,), (1,)), ((), ())), preferred_element_type=F32)


def nn(a, b):
    return lax.dot_general(a, b, (((1,), (0,)), ((), ())), preferred_element_type=F32)


def next_row(value, period):
    rows = value.shape[0]
    rolled = pltpu.roll(value, rows - 1, 0)
    row = lax.broadcasted_iota(jnp.int32, value.shape, 0)
    return jnp.where(row % period == period - 1, 0.0, rolled)


def pack_kernel(pre_ref, og_ref, hx_ref, hy_ref, hc_ref, sems):
    copies = []

    def copy(src, dst):
        copies.append(pltpu.make_async_copy(src, dst, sems.at[len(copies)]))
        copies[-1].start()

    for j in range(CY):
        copy(og_ref.at[0, 0, j], hx_ref.at[pl.ds(j * CZ, CZ)])
    for y in range(MY):
        copy(pre_ref.at[0, 0, y], hx_ref.at[pl.ds(CY * CZ + y * MZ, MZ)])
    copy(og_ref.at[0, 0, 0], hy_ref.at[pl.ds(0, CZ)])
    for x in range(MX):
        copy(pre_ref.at[0, x, 0], hy_ref.at[pl.ds(CZ + x * MZ, MZ)])
    copy(og_ref.at[0, 0, 0], hc_ref.at[pl.ds(0, CZ)])
    copy(pre_ref.at[0, 0, 0], hc_ref.at[pl.ds(CZ, MZ)])
    for c in copies:
        c.wait()


def prep_kernel(
    u_hbm, pre_hbm, og_hbm, w1_hbm, w2_hbm,
    r1_ref, r2_ref, u1t_ref, u2t_ref, pre_ref, og_ref,
    u_ref, w1_ref, w2_ref, act_s, sems,
):
    w1_copy, w2_copy, pre_copy, u_copy, og_copy = [
        pltpu.make_async_copy(source, target, sems.at[k])
        for k, (source, target) in enumerate(
            ((w1_hbm, w1_ref), (w2_hbm, w2_ref), (pre_hbm, pre_ref), (u_hbm, u_ref), (og_hbm, og_ref))
        )
    ]
    for copy in (w1_copy, w2_copy, pre_copy, u_copy, og_copy):
        copy.start()
    w1_copy.wait()
    zero = jnp.zeros((CIN, C1), BF)
    for kx in range(3):
        for ky in range(3):
            at = SLOT[ky] * 2 * CIN
            r1_ref[kx, at : at + CIN, 0:C1] = w1_ref[kx, ky, 1]
            r1_ref[kx, at : at + CIN, C1:] = zero
            r1_ref[kx, at + CIN : at + 2 * CIN, 0:C1] = w1_ref[kx, ky, 2]
            r1_ref[kx, at + CIN : at + 2 * CIN, C1:] = w1_ref[kx, ky, 0]

    w2_copy.wait()
    zero = jnp.zeros((C1, C2), BF)
    for kx in range(3):
        for ky in range(3):
            t = kx * 3 + ky
            r2_ref[t, 0:C1, 0:C2] = w2_ref[kx, ky, 1]
            r2_ref[t, 0:C1, C2:] = zero
            r2_ref[t, C1:, 0:C2] = w2_ref[kx, ky, 2]
            r2_ref[t, C1:, C2:] = w2_ref[kx, ky, 0]

    pre_copy.wait()
    own = MY * MZ
    for mx in range(MX):
        pre = pre_ref[0, mx].reshape(own, C1).astype(F32)
        act_s[mx * own : (mx + 1) * own, :] = jnp.where(pre > 0, pre, 0.3 * pre)
    for px in range(2):
        for py in range(2):
            for s in range(2):
                rows = [
                    act_s[pl.ds((px * MY + 2 * j + py) * MZ + s, CZ, stride=2), :]
                    for j in range(CY)
                ]
                u2t_ref[px * 2 + py, s * C1 : (s + 1) * C1, :] = jnp.concatenate(rows, 0).T.astype(BF)

    u_copy.wait()
    for px in range(2):
        for py in range(2):
            for i in range(MX):
                for j in range(0, MY, 2):
                    pair = jnp.concatenate(
                        [u_ref[0, 2 * i + px, 2 * (j + e) + py] for e in range(2)], 0
                    )
                    at = (i * MY + j) * MZ
                    u1t_ref[px * 2 + py, :, at : at + 2 * MZ] = pair.T
    og_copy.wait()


def share(buf_s, keep_ref, send_ref, rows):
    core = lax.axis_index("core")
    keep_ref[...] = buf_s[pl.ds(pl.multiple_of(core * rows, rows), rows), :]
    send_ref[...] = buf_s[pl.ds(pl.multiple_of((1 - core) * rows, rows), rows), :]


def main_kernel(
    pre_ref, og_ref, hx_ref, hy_ref, hc_ref, r2_ref, u2t_ref,
    a_ref, keep_ref, send_ref,
    b_s, ga_s, buf_s,
):
    def put_b(at, value):
        n = value.shape[0]
        b_s[at : at + n, 0:C2] = value
        b_s[at : at + n, C2:] = next_row(value.astype(F32), CZ).astype(BF)

    def inside(value, edge):
        return jnp.where(edge > 0, 0.0, value.astype(F32)).astype(BF)

    edge_x = (lax.axis_index(AX) == lax.axis_size(AX) - 1).astype(jnp.int32)
    edge_y = (lax.axis_index(AZ) == lax.axis_size(AZ) - 1).astype(jnp.int32)
    put_b(0, og_ref[0, 0].reshape(CY * CZ, C2))
    put_b(CY * CZ, inside(hy_ref[0:CZ], edge_y))
    put_b((CY + 1) * CZ, inside(hx_ref[0 : CY * CZ], edge_x))
    put_b((2 * CY + 1) * CZ, inside(hc_ref[0:CZ], edge_x + edge_y))

    def put_ga(mx, my, value):
        base = (mx * EY + my) * MZ
        ga_s[pl.ds(base, CZ, stride=2), :] = value[:, 0:C1]
        ga_s[pl.ds(base + 1, CZ, stride=2), :] = value[:, C1:]

    def b_rows(i, j, n):
        at = (i * (CY + 1) + j) * CZ
        return b_s[at : at + n * CZ, :]

    for px in range(2):
        for i in range(2 - px):
            for py in range(2):
                n = CY + 1 - py
                total = None
                for kx, dx in TAPS[px]:
                    for ky, dy in TAPS[py]:
                        part = nt(b_rows(i + dx, dy, n), r2_ref[kx * 3 + ky])
                        total = part if total is None else total + part
                for j in range(n):
                    put_ga(2 * i + px, 2 * j + py, total[j * CZ : (j + 1) * CZ])

    def put_a(at, pre):
        n = pre.shape[0]
        slope = jnp.where(pre.astype(F32) > 0, 1.0, 0.3)
        value = ga_s[at : at + n, :] * slope
        a_ref[at : at + n, 0:C1] = value.astype(BF)
        a_ref[at : at + n, C1:] = next_row(value, MZ).astype(BF)

    own = MY * MZ
    for mx in range(MX):
        put_a(mx * EY * MZ, pre_ref[0, mx].reshape(own, C1))
        put_a((mx * EY + MY) * MZ, hy_ref[CZ + mx * MZ : CZ + (mx + 1) * MZ])
    put_a(MX * EY * MZ, hx_ref[CY * CZ : CY * CZ + own])
    put_a((MX * EY + MY) * MZ, hc_ref[CZ : CZ + MZ])

    for kx in range(3):
        px, dx = TAP[kx]
        for ky in range(3):
            py, dy = TAP[ky]
            d = nn(u2t_ref[px * 2 + py], b_rows(dx, dy, CY)) * SCALE_TWO
            at = (kx * 3 + ky) * 3 * C1
            buf_s[at : at + C1, :] = d[C1:, C2:].astype(BF)
            buf_s[at + C1 : at + 2 * C1, :] = d[0:C1, 0:C2].astype(BF)
            buf_s[at + 2 * C1 : at + 3 * C1, :] = d[C1:, 0:C2].astype(BF)

    share(buf_s, keep_ref, send_ref, ROWS_TWO // 2)


def one_kernel(a_ref, u1t_ref, keep_ref, send_ref, buf_s):
    own = MY * MZ
    for kx in range(3):
        px, dx = TAP[kx]
        for ky in range(3):
            py, dy = TAP[ky]
            total = None
            for i in range(MX):
                at = ((i + dx) * EY + dy) * MZ
                part = nn(
                    u1t_ref[px * 2 + py, :, i * own : (i + 1) * own], a_ref[at : at + own, :]
                )
                total = part if total is None else total + part
            d = total * SCALE_ONE
            at = (kx * 3 + ky) * 3 * CIN
            buf_s[at : at + CIN, :] = d[CIN:, C1:].astype(BF)
            buf_s[at + CIN : at + 2 * CIN, :] = d[0:CIN, 0:C1].astype(BF)
            buf_s[at + 2 * CIN : at + 3 * CIN, :] = d[CIN:, 0:C1].astype(BF)

    share(buf_s, keep_ref, send_ref, ROWS_ONE // 2)


def join_kernel(keep_two, got_two, keep_one, got_one, half_ref):
    two = ROWS_TWO // 2
    both = two + ROWS_ONE // 2
    half_ref[0:two] = (keep_two[...].astype(F32) + got_two[...].astype(F32)).astype(BF)
    half_ref[two:both] = (keep_one[...].astype(F32) + got_one[...].astype(F32)).astype(BF)
    half_ref[both:] = jnp.zeros((HALF - both, C1), BF)


def input_kernel(a_ref, r1_ref, out_ref):
    wide = 2 * CIN
    step = 4
    for i in range(MX):
        for px in range(2):
            for j in range(0, MY, step):
                both = None
                odd = None
                for kx, dx in TAPS[px]:
                    at = ((i + dx) * EY + j) * MZ
                    part = nt(a_ref[at : at + step * MZ, :], r1_ref[kx, 0 : 2 * wide, :])
                    both = part if both is None else both + part
                    part = nt(a_ref[at + MZ : at + (step + 1) * MZ, :], r1_ref[kx, 2 * wide :, :])
                    odd = part if odd is None else odd + part
                even = both[:, 0:wide].astype(BF)
                odd = (both[:, wide:] + odd).astype(BF)
                for e in range(step):
                    rows = slice(e * MZ, (e + 1) * MZ)
                    out_ref[0, 2 * i + px, 2 * (j + e)] = even[rows]
                    out_ref[0, 2 * i + px, 2 * (j + e) + 1] = odd[rows]


def output_kernel(second, half_ref, *refs):
    one_hbm, two_hbm, wide, sems = refs[-4:]
    core = lax.axis_index("core")
    core = 1 - core if second else core
    copies = []
    for k in range(3):
        target, rows = ((two_hbm, ROWS_TWO // 4), (two_hbm, ROWS_TWO // 4), (one_hbm, ROWS_ONE // 2))[k]
        at = k * (ROWS_TWO // 4)
        wide[at : at + rows] = half_ref[at : at + rows].astype(F32)
        start = core * (ROWS_TWO // 2) + at if k < 2 else core * rows
        copies.append(
            pltpu.make_async_copy(
                wide.at[pl.ds(at, rows)],
                target.at[pl.ds(pl.multiple_of(start, 8), rows)],
                sems.at[k],
            )
        )
        copies[-1].start()
    for copy in copies:
        copy.wait()


def vmem(n):
    return [pl.BlockSpec(memory_space=pltpu.VMEM)] * n


def hbm(n):
    return [pl.BlockSpec(memory_space=pltpu.HBM)] * n


def far(*arrays):
    return [pltpu.with_memory_space_constraint(x, pltpu.HBM) for x in arrays]


LIMIT = 20 * 1024 * 1024


def call(kernel, out, scratch, in_specs, flops, bytes_moved):
    return pl.pallas_call(
        kernel,
        out_shape=tuple(out),
        in_specs=in_specs,
        out_specs=tuple(vmem(len(out))),
        scratch_shapes=scratch,
        cost_estimate=pl.CostEstimate(flops=flops, bytes_accessed=bytes_moved, transcendentals=0),
        compiler_params=pltpu.CompilerParams(vmem_limit_bytes=LIMIT),
    )


def pack_call(pre, og):
    out = [pltpu.VMEM(((CY * CZ + MY * MZ), C1), BF), pltpu.VMEM((CZ + MX * MZ, C1), BF), pltpu.VMEM((CZ + MZ, C1), BF)]
    count = CY + MY + 1 + MX + 2
    return call(pack_kernel, out, [pltpu.SemaphoreType.DMA((count,))], hbm(2), 0, 500_000)(*far(pre, og))


def prep_call(u, pre, og, w1, w2):
    out = [
        pltpu.VMEM((3, 6 * CIN, 2 * C1), BF),
        pltpu.VMEM((9, 2 * C1, 2 * C2), BF),
        pltpu.VMEM((4, 2 * CIN, MX * MY * MZ), BF),
        pltpu.VMEM((4, 2 * C1, CY * CZ), BF),
        pltpu.VMEM(pre.shape, BF),
        pltpu.VMEM(og.shape, BF),
    ]
    scratch = [
        pltpu.VMEM(u.shape, BF),
        pltpu.VMEM(w1.shape, BF),
        pltpu.VMEM(w2.shape, BF),
        pltpu.VMEM((MX * MY * MZ, C1), F32),
        pltpu.SemaphoreType.DMA((5,)),
    ]
    return call(prep_kernel, out, scratch, hbm(5), 0, 6_000_000)(*far(u, pre, og, w1, w2))


def main_call(pre, og, hx, hy, hc, r2, u2t):
    out = [
        pltpu.VMEM((EX * EY * MZ, 2 * C1), BF),
        pltpu.VMEM((ROWS_TWO // 2, C1), BF),
        pltpu.VMEM((ROWS_TWO // 2, C1), BF),
    ]
    scratch = [
        pltpu.VMEM((2 * (CY + 1) * CZ, 2 * C2), BF),
        pltpu.VMEM((EX * EY * MZ, C1), F32),
        pltpu.VMEM((ROWS_TWO, C1), BF),
    ]
    return call(main_kernel, out, scratch, vmem(7), 800_000_000, 4_000_000)(
        pre, og, hx, hy, hc, r2, u2t
    )


def one_call(a, u1t):
    out = [pltpu.VMEM((ROWS_ONE // 2, C1), BF), pltpu.VMEM((ROWS_ONE // 2, C1), BF)]
    scratch = [pltpu.VMEM((ROWS_ONE, C1), BF)]
    return call(one_kernel, out, scratch, vmem(2), 1_200_000_000, 3_000_000)(a, u1t)


def join_call(*parts):
    return call(join_kernel, [pltpu.VMEM((HALF, C1), BF)], [], vmem(4), 0, 2_000_000)(*parts)[0]


def input_call(a, r1):
    out = [jax.ShapeDtypeStruct((1, 2 * MX, 2 * MY, MZ, 2 * CIN), BF)]
    return call(input_kernel, out, [], vmem(2), 1_200_000_000, 3_000_000)(a, r1)[0]


def output_call(half, before=()):
    second = len(before) // 2
    return pl.pallas_call(
        functools.partial(output_kernel, second),
        out_shape=(
            jax.ShapeDtypeStruct((ROWS_ONE, C1), F32),
            jax.ShapeDtypeStruct((ROWS_TWO, C1), F32),
        ),
        in_specs=vmem(1) + hbm(len(before)),
        out_specs=tuple(hbm(2)),
        scratch_shapes=[pltpu.VMEM((HALF, C1), F32), pltpu.SemaphoreType.DMA((3,))],
        input_output_aliases={1: 0, 2: 1} if second else {},
        cost_estimate=pl.CostEstimate(flops=0, bytes_accessed=2_000_000, transcendentals=0),
        compiler_params=pltpu.CompilerParams(vmem_limit_bytes=LIMIT),
        name="output",
    )(half, *before)


def backward(u, pre, og, w1, w2):
    sx = lax.axis_size("y") * lax.axis_size("xl")
    sz = lax.axis_size("zh") * lax.axis_size("zl")
    from_x = [((i + 1) % sx, i) for i in range(sx)]
    from_z = [((i + 1) % sz, i) for i in range(sz)]
    from_xz = [
        ((i + 1) % sx * sz + (j + 1) % sz, i * sz + j) for i in range(sx) for j in range(sz)
    ]
    hx, hy, hc = pack_call(pre, og)
    hx = lax.ppermute(hx, AX, from_x)
    hc = lax.ppermute(hc, AX + AZ, from_xz)
    hy = lax.ppermute(hy, AZ, from_z)
    r1, r2, u1t, u2t, pre, og = prep_call(u, pre, og, w1, w2)
    swap = [(0, 1), (1, 0)]
    a, keep_two, send_two = main_call(pre, og, hx, hy, hc, r2, u2t)
    got_two = lax.ppermute(send_two, "core", swap)
    keep_one, send_one = one_call(a, u1t)
    got_one = lax.ppermute(send_one, "core", swap)
    half = join_call(keep_two, got_two, keep_one, got_one)

    group = ("xh", "xl", "zl", "y")
    parts = lax.all_to_all(half.reshape(GROUP, CHUNK, C1), group, 0, 0, tiled=True)
    grad_input = input_call(a, r1)
    chunk = jnp.sum(parts.astype(F32), axis=0).astype(BF)
    far = lax.ppermute(chunk, "zh", [((i + 2) % 4, i) for i in range(4)])
    up = lax.ppermute(chunk, "zh", [((i + 1) % 4, i) for i in range(4)])
    down = lax.ppermute(chunk, "zh", [((i + 3) % 4, i) for i in range(4)])
    chunk = (chunk.astype(F32) + far.astype(F32)) + (up.astype(F32) + down.astype(F32))
    chunk = jnp.broadcast_to(chunk.astype(BF)[None], (GROUP, CHUNK, C1))
    mine = lax.all_to_all(chunk, group, 0, 0, tiled=True).reshape(HALF, C1)
    other = lax.ppermute(mine, "core", swap)
    grad_one, grad_two = output_call(other, output_call(mine))
    return grad_input, grad_one.reshape(3, 3, 3, CIN, C1), grad_two.reshape(3, 3, 3, C1, C2)


def solution(mesh):
    fine = Mesh(mesh.devices.reshape(2, 2, 4, 2, 4, 2), ("xh", "core", "y", "xl", "zh", "zl"))
    spec = P(("xh", "core"), ("y", "xl"), ("zh", "zl"), None, None)
    return jax.shard_map(
        backward,
        mesh=fine,
        in_specs=(spec, spec, spec, P(), P()),
        out_specs=(spec, P(), P()),
        check_vma=False,
    )
```

profile of v0, /device:TPU:1, one launch (start us, length us, event | category | flops | bytes accessed | tf_op | source)
XLA Modules:
  0.0 72.9 jit_solution(15597636189654912778)
XLA Ops:
  0.6 1.1 %shard_map.77 = (bf16[640,128]{1,0:T(8,128)(2,1)S(1)}, bf16[160,128]{1,0:T(8,128)(2,1)S(1)}, bf16[96,128]{1,0:T(8,128)(2,1)S(1)}) custom-call(bf16[1,2,8,64,128]{4,3,2,1,0:T(8,128)(2,1)} %pre_ref.1, bf16[1,1,4,32,128]{4,3,2,1,0:T(8,128)(2,1)} %og_ref.1), custom_call_target="tpu_custom_call" | custom-call | bytes 500000 | tf_op jit(solution)/shard_map/pallas_call | solution.py:307
  1.7 4.6 %collective-permute-start = (bf16[640,128]{1,0:T(8,128)(2,1)S(1)}, bf16[640,128]{1,0:T(8,128)(2,1)S(1)}, u32[]{:S(2)}, u32[]{:S(2)}) collective-permute-start(bf16[640,128]{1,0:T(8,128)(2,1)S(1)} %get-tuple-element.23), channel_id=1, source_target_pairs={{8,0},{16,8},{24,16},{32,24},{40,32},{48,40},{56,48},{0,56},{9,1},... | collective-permute-start | bytes 491528 | tf_op jit(solution)/shard_map/ppermute | solution.py:387
  6.3 5.6 %collective-permute-start.1 = (bf16[160,128]{1,0:T(8,128)(2,1)S(1)}, bf16[160,128]{1,0:T(8,128)(2,1)S(1)}, u32[]{:S(2)}, u32[]{:S(2)}) collective-permute-start(bf16[160,128]{1,0:T(8,128)(2,1)S(1)} %get-tuple-element.24), channel_id=1, source_target_pairs={{1,0},{2,1},{3,2},{4,3},{5,4},{6,5},{7,6},{0,7},{9,8},{10,9},{11,1... | collective-permute-start | bytes 122888 | tf_op jit(solution)/shard_map/ppermute | solution.py:389
  11.8 0.7 collective-permute-start.2
  12.5 2.1 %shard_map.76 = (bf16[3,384,256]{2,1,0:T(8,128)(2,1)S(1)}, bf16[9,256,256]{2,1,0:T(8,128)(2,1)S(1)}, bf16[4,128,1024]{2,1,0:T(8,128)(2,1)S(1)}, bf16[4,256,128]{...) custom-call(bf16[1,4,16,64,128]{4,3,2,1,0:T(8,128)(2,1)} %u_hbm.1, ...), custom_call_target="tpu_custom_call" | custom-call | bytes 6000000 | tf_op jit(solution)/shard_map/pallas_call | solution.py:326
  14.6 0.8 %collective-permute-done.2.hc_ref = bf16[96,128]{1,0:T(8,128)(2,1)S(1)} collective-permute-done((bf16[96,128]{1,0:T(8,128)(2,1)S(1)}, bf16[96,128]{1,0:T(8,128)(2,1)S(1)}, u32[]{:S(2)}, u32[]{:S(2)}) %collective-permute-start.2) | collective-permute-done | bytes 24608 | tf_op jit(solution)/shard_map/ppermute | solution.py:388
  15.4 0.0 collective-permute-done.1.hy_ref
  15.4 0.0 collective-permute-done.hx_ref
  15.4 1.2 %shard_map.78 = (bf16[1728,256]{1,0:T(8,128)(2,1)S(1)}, bf16[1728,128]{1,0:T(8,128)(2,1)S(1)}, bf16[1728,128]{1,0:T(8,128)(2,1)S(1)}) custom-call(bf16[1,2,8,64,128]{4,3,2,1,0:T(8,128)(2,1)S(1)} %get-tuple-element.21.pre_ref, bf16[1,1,4,32,128]{4,3,2,1,0:T(8,128)(2,1)S(1)} %get-tuple-element.22.og_ref, bf16[640,128]{1,0:T(8,128)(2,1)S(1)} %collective-permute-done.hx_ref, ...), custom_call_target="tpu_custom_call" | custom-call | flops 800000000 | bytes 4000000 | tf_op jit(solution)/shard_map/pallas_call | solution.py:340
  16.6 2.5 %collective-permute-start.3 = (bf16[1728,128]{1,0:T(8,128)(2,1)S(1)}, bf16[1728,128]{1,0:T(8,128)(2,1)S(1)}, u32[]{:S(2)}, u32[]{:S(2)}) collective-permute-start(bf16[1728,128]{1,0:T(8,128)(2,1)S(1)} %get-tuple-element.31), channel_id=1, source_target_pairs={{0,64},{64,0},{1,65},{65,1},{2,66},{66,2},{3,67},{67,3},{4,68},{68... | collective-permute-start | bytes 1327112 | tf_op jit(solution)/shard_map/ppermute | solution.py:393
  19.0 0.8 %shard_map.80 = (bf16[864,128]{1,0:T(8,128)(2,1)S(1)}, bf16[864,128]{1,0:T(8,128)(2,1)S(1)}) custom-call(bf16[1728,256]{1,0:T(8,128)(2,1)S(1)} %get-tuple-element.28.a_ref, bf16[4,128,1024]{2,1,0:T(8,128)(2,1)S(1)} %get-tuple-element.32.u1t_ref), custom_call_target="tpu_custom_call" | custom-call | flops 1200000000 | bytes 3000000 | tf_op jit(solution)/shard_map/pallas_call | solution.py:348
  19.9 0.1 collective-permute-start.4
  20.0 1.5 %collective-permute-done.4.got_one = bf16[864,128]{1,0:T(8,128)(2,1)S(1)} collective-permute-done((bf16[864,128]{1,0:T(8,128)(2,1)S(1)}, bf16[864,128]{1,0:T(8,128)(2,1)S(1)}, u32[]{:S(2)}, u32[]{:S(2)}) %collective-permute-start.4) | collective-permute-done | bytes 221216 | tf_op jit(solution)/shard_map/ppermute | solution.py:395
  21.5 0.0 collective-permute-done.3.got_two
  21.5 0.2 shard_map.81
  21.6 17.9 %all_to_all.10 = bf16[32,88,128]{2,1,0:T(8,128)(2,1)S(1)} all-to-all(bf16[32,88,128]{2,1,0:T(8,128)(2,1)S(1)} %bitcast.6), channel_id=1, replica_groups=mesh['xh'=2,'core'=2,'y'=4,'xl'=2,'zh'=4,'zl'=2] {'xh','xl','zl','y'}, dimensions={0} | all-to-all | bytes 1441792 | tf_op jit(solution)/shard_map/all_to_all | solution.py:399
  39.5 0.1 reduce_sum.12
  39.6 0.1 collective-permute-start.7
  39.7 3.6 %collective-permute-start.6 = (bf16[88,128]{1,0:T(8,128)(2,1)S(1)}, bf16[88,128]{1,0:T(8,128)(2,1)S(1)}, u32[]{:S(2)}, u32[]{:S(2)}) collective-permute-start(bf16[88,128]{1,0:T(8,128)(2,1)S(1)} %reduce_sum.12), channel_id=1, source_target_pairs={{2,0},{4,2},{6,4},{0,6},{3,1},{5,3},{7,5},{1,7},{10,8},{12,10},{14... | collective-permute-start | bytes 67592 | tf_op jit(solution)/shard_map/ppermute | solution.py:403
  43.3 2.5 %collective-permute-start.5 = (bf16[88,128]{1,0:T(8,128)(2,1)S(1)}, bf16[88,128]{1,0:T(8,128)(2,1)S(1)}, u32[]{:S(2)}, u32[]{:S(2)}) collective-permute-start(bf16[88,128]{1,0:T(8,128)(2,1)S(1)} %reduce_sum.12), channel_id=1, source_target_pairs={{4,0},{6,2},{0,4},{2,6},{5,1},{7,3},{1,5},{3,7},{12,8},{14,10},{8,... | collective-permute-start | bytes 67592 | tf_op jit(solution)/shard_map/ppermute | solution.py:402
  45.8 0.0 collective-permute-done.7
  45.8 0.0 collective-permute-done.6
  45.8 4.0 %collective-permute-done.5 = bf16[88,128]{1,0:T(8,128)(2,1)S(1)} collective-permute-done((bf16[88,128]{1,0:T(8,128)(2,1)S(1)}, bf16[88,128]{1,0:T(8,128)(2,1)S(1)}, u32[]{:S(2)}, u32[]{:S(2)}) %collective-permute-start.5) | collective-permute-done | bytes 22560 | tf_op jit(solution)/shard_map/ppermute | solution.py:402
  49.9 0.1 broadcast_in_dim.2
  50.0 14.4 %all_to_all.11 = bf16[32,88,128]{2,1,0:T(8,128)(2,1)S(1)} all-to-all(bf16[32,88,128]{2,1,0:T(8,128)(2,1)S(1)} %broadcast_in_dim.2), channel_id=1, replica_groups=mesh['xh'=2,'core'=2,'y'=4,'xl'=2,'zh'=4,'zl'=2] {'xh','xl','zl','y'}, dimensions={0} | all-to-all | bytes 1441792 | tf_op jit(solution)/shard_map/all_to_all | solution.py:407
  64.4 4.4 %collective-permute-start.8 = (bf16[2816,128]{1,0:T(8,128)(2,1)S(1)}, bf16[2816,128]{1,0:T(8,128)(2,1)S(1)}, u32[]{:S(2)}, u32[]{:S(2)}) collective-permute-start(bf16[2816,128]{1,0:T(8,128)(2,1)S(1)} %bitcast.4), channel_id=1, source_target_pairs={{0,64},{64,0},{1,65},{65,1},{2,66},{66,2},{3,67},{67,3},{4,68},{68... | collective-permute-start | bytes 2162696 | tf_op jit(solution)/shard_map/ppermute | solution.py:408
  68.7 2.0 %shard_map.79 = bf16[1,4,16,64,128]{4,3,2,1,0:T(8,128)(2,1)} custom-call(bf16[1728,256]{1,0:T(8,128)(2,1)S(1)} %get-tuple-element.28.a_ref, bf16[3,384,256]{2,1,0:T(8,128)(2,1)S(1)} %get-tuple-element.29.r1_ref), custom_call_target="tpu_custom_call" | custom-call | flops 1200000000 | bytes 3000000 | tf_op jit(solution)/shard_map/pallas_call | solution.py:357
  70.7 1.1 %output.2 = (f32[1728,128]{1,0:T(8,128)}, f32[3456,128]{1,0:T(8,128)}) custom-call(bf16[2816,128]{1,0:T(8,128)(2,1)S(1)} %bitcast.5), custom_call_target="tpu_custom_call" | custom-call | bytes 2000000 | tf_op jit(solution)/shard_map/output/pallas_call | solution.py:362
  71.8 0.0 collective-permute-done.8.half_ref
  71.8 1.1 %output.3 = (f32[1728,128]{1,0:T(8,128)}, f32[3456,128]{1,0:T(8,128)}) custom-call(bf16[2816,128]{1,0:T(8,128)(2,1)S(1)} %collective-permute-done.8.half_ref, f32[1728,128]{1,0:T(8,128)} %get-tuple-element.35.refs_0_, f32[3456,128]{1,0:T(8,128)} %get-tuple-element.36.refs_1_), custom_call_target="tpu_custom_call", output_to_operand_aliasing={{0}: (1, {}), {1}: (2, {})} | custom-call | bytes 2000000 | tf_op jit(solution)/shard_map/output/pallas_call | solution.py:362
  (1 shorter events, 0.0 us)
Async XLA Ops:
  1.7 13.7 %collective-permute-start = (bf16[640,128]{1,0:T(8,128)(2,1)S(1)}, bf16[640,128]{1,0:T(8,128)(2,1)S(1)}, u32[]{:S(2)}, u32[]{:S(2)}) collective-permute-start(bf16[640,128]{1,0:T(8,128)(2,1)S(1)} %get-tuple-element.23), channel_id=1, source_target_pairs={{8,0},{16,8},{24,16},{32,24},{40,32},{48,40},{56,48},{0,56},{9,1},... | collective-permute-start | bytes 491528 | tf_op jit(solution)/shard_map/ppermute | solution.py:387
  6.3 9.2 %collective-permute-start.1 = (bf16[160,128]{1,0:T(8,128)(2,1)S(1)}, bf16[160,128]{1,0:T(8,128)(2,1)S(1)}, u32[]{:S(2)}, u32[]{:S(2)}) collective-permute-start(bf16[160,128]{1,0:T(8,128)(2,1)S(1)} %get-tuple-element.24), channel_id=1, source_target_pairs={{1,0},{2,1},{3,2},{4,3},{5,4},{6,5},{7,6},{0,7},{9,8},{10,9},{11,1... | collective-permute-start | bytes 122888 | tf_op jit(solution)/shard_map/ppermute | solution.py:389
  11.8 3.6 %collective-permute-start.2 = (bf16[96,128]{1,0:T(8,128)(2,1)S(1)}, bf16[96,128]{1,0:T(8,128)(2,1)S(1)}, u32[]{:S(2)}, u32[]{:S(2)}) collective-permute-start(bf16[96,128]{1,0:T(8,128)(2,1)S(1)} %get-tuple-element.25), channel_id=1, source_target_pairs={{9,0},{10,1},{11,2},{12,3},{13,4},{14,5},{15,6},{8,7},{17,8},{18,9... | collective-permute-start | bytes 73736 | tf_op jit(solution)/shard_map/ppermute | solution.py:388
  16.6 4.9 %collective-permute-start.3 = (bf16[1728,128]{1,0:T(8,128)(2,1)S(1)}, bf16[1728,128]{1,0:T(8,128)(2,1)S(1)}, u32[]{:S(2)}, u32[]{:S(2)}) collective-permute-start(bf16[1728,128]{1,0:T(8,128)(2,1)S(1)} %get-tuple-element.31), channel_id=1, source_target_pairs={{0,64},{64,0},{1,65},{65,1},{2,66},{66,2},{3,67},{67,3},{4,68},{68... | collective-permute-start | bytes 1327112 | tf_op jit(solution)/shard_map/ppermute | solution.py:393
  19.9 1.6 %collective-permute-start.4 = (bf16[864,128]{1,0:T(8,128)(2,1)S(1)}, bf16[864,128]{1,0:T(8,128)(2,1)S(1)}, u32[]{:S(2)}, u32[]{:S(2)}) collective-permute-start(bf16[864,128]{1,0:T(8,128)(2,1)S(1)} %get-tuple-element.34), channel_id=1, source_target_pairs={{0,64},{64,0},{1,65},{65,1},{2,66},{66,2},{3,67},{67,3},{4,68},{68... | collective-permute-start | bytes 663560 | tf_op jit(solution)/shard_map/ppermute | solution.py:395
  39.6 6.2 %collective-permute-start.7 = (bf16[88,128]{1,0:T(8,128)(2,1)S(1)}, bf16[88,128]{1,0:T(8,128)(2,1)S(1)}, u32[]{:S(2)}, u32[]{:S(2)}) collective-permute-start(bf16[88,128]{1,0:T(8,128)(2,1)S(1)} %reduce_sum.12), channel_id=1, source_target_pairs={{6,0},{0,2},{2,4},{4,6},{7,1},{1,3},{3,5},{5,7},{14,8},{8,10},{10,... | collective-permute-start | bytes 67592 | tf_op jit(solution)/shard_map/ppermute | solution.py:404
  39.7 6.1 %collective-permute-start.6 = (bf16[88,128]{1,0:T(8,128)(2,1)S(1)}, bf16[88,128]{1,0:T(8,128)(2,1)S(1)}, u32[]{:S(2)}, u32[]{:S(2)}) collective-permute-start(bf16[88,128]{1,0:T(8,128)(2,1)S(1)} %reduce_sum.12), channel_id=1, source_target_pairs={{2,0},{4,2},{6,4},{0,6},{3,1},{5,3},{7,5},{1,7},{10,8},{12,10},{14... | collective-permute-start | bytes 67592 | tf_op jit(solution)/shard_map/ppermute | solution.py:403
  43.3 6.6 %collective-permute-start.5 = (bf16[88,128]{1,0:T(8,128)(2,1)S(1)}, bf16[88,128]{1,0:T(8,128)(2,1)S(1)}, u32[]{:S(2)}, u32[]{:S(2)}) collective-permute-start(bf16[88,128]{1,0:T(8,128)(2,1)S(1)} %reduce_sum.12), channel_id=1, source_target_pairs={{4,0},{6,2},{0,4},{2,6},{5,1},{7,3},{1,5},{3,7},{12,8},{14,10},{8,... | collective-permute-start | bytes 67592 | tf_op jit(solution)/shard_map/ppermute | solution.py:402
  64.4 7.4 %collective-permute-start.8 = (bf16[2816,128]{1,0:T(8,128)(2,1)S(1)}, bf16[2816,128]{1,0:T(8,128)(2,1)S(1)}, u32[]{:S(2)}, u32[]{:S(2)}) collective-permute-start(bf16[2816,128]{1,0:T(8,128)(2,1)S(1)} %bitcast.4), channel_id=1, source_target_pairs={{0,64},{64,0},{1,65},{65,1},{2,66},{66,2},{3,67},{67,3},{4,68},{68... | collective-permute-start | bytes 2162696 | tf_op jit(solution)/shard_map/ppermute | solution.py:408
where the time goes:
time: 73.3 us; the launch traced here: 72.9 us
  blocking collectives  32.3 us (44%)
  starting transfers between devices  23.9 us (33%)
  Pallas kernels  9.49 us (13%)
  waiting for transfers between devices  6.31 us (9%)
    all_to_all x1, blocking collectives, backward(): lax.all_to_all(half.reshape(GROUP, CHUNK, C1), group, 0, 0, tiled=True)  17.9 us
    all_to_all x1, blocking collectives, backward(): mine = lax.all_to_all(chunk, group, 0, 0, tiled=True).reshape(HALF, C1)  14.4 us
    ppermute x1, starting transfers between devices, backward(): hy = lax.ppermute(hy, AZ, from_z)  5.58 us
    ppermute x1, starting transfers between devices, backward(): hx = lax.ppermute(hx, AX, from_x)  4.56 us
    ppermute x1, starting transfers between devices, backward(): other = lax.ppermute(mine, 'core', swap)  4.35 us
    ppermute x1, waiting for transfers between devices, backward(): far = lax.ppermute(chunk, 'zh', [((i + 2) % 4, i) for i in range(4)])  4.04 us
    ppermute x1, starting transfers between devices, backward(): up = lax.ppermute(chunk, 'zh', [((i + 1) % 4, i) for i in range(4)])  3.56 us
    ppermute x1, starting transfers between devices, backward(): far = lax.ppermute(chunk, 'zh', [((i + 2) % 4, i) for i in range(4)])  2.52 us
  transfers between devices with their start and end apart: 9, of which 3 were waited for; matrix products, arithmetic and copies ran while one was open for 0% of the time, Pallas kernels for 8%

commit v1 on v0

--- a/solution.py
+++ b/solution.py
@@ -320,7 +320,7 @@
         pltpu.VMEM(u.shape, BF),
         pltpu.VMEM(w1.shape, BF),
         pltpu.VMEM(w2.shape, BF),
-        pltpu.VMEM((MX * MY * MZ, C1), F32),
+        pltpu.VMEM((MX * MY * MZ + 8, C1), F32),
         pltpu.SemaphoreType.DMA((5,)),
     ]
     return call(prep_kernel, out, scratch, hbm(5), 0, 6_000_000)(*far(u, pre, og, w1, w2))
@@ -334,7 +334,7 @@
     ]
     scratch = [
         pltpu.VMEM((2 * (CY + 1) * CZ, 2 * C2), BF),
-        pltpu.VMEM((EX * EY * MZ, C1), F32),
+        pltpu.VMEM((EX * EY * MZ + 8, C1), F32),
         pltpu.VMEM((ROWS_TWO, C1), BF),
     ]
     return call(main_kernel, out, scratch, vmem(7), 800_000_000, 4_000_000)(
@@ -399,9 +399,9 @@
     parts = lax.all_to_all(half.reshape(GROUP, CHUNK, C1), group, 0, 0, tiled=True)
     grad_input = input_call(a, r1)
     chunk = jnp.sum(parts.astype(F32), axis=0).astype(BF)
-    far = lax.ppermute(chunk, "zh", [((i + 2) % 4, i) for i in range(4)])
-    up = lax.ppermute(chunk, "zh", [((i + 1) % 4, i) for i in range(4)])
-    down = lax.ppermute(chunk, "zh", [((i + 3) % 4, i) for i in range(4)])
+    far = lax.ppermute(chunk, "zh", [(i ^ 2, i) for i in range(4)])
+    up = lax.ppermute(chunk, "zh", [(i ^ 1, i) for i in range(4)])
+    down = lax.ppermute(chunk, "zh", [(i ^ 3, i) for i in range(4)])
     chunk = (chunk.astype(F32) + far.astype(F32)) + (up.astype(F32) + down.astype(F32))
     chunk = jnp.broadcast_to(chunk.astype(BF)[None], (GROUP, CHUNK, C1))
     mine = lax.all_to_all(chunk, group, 0, 0, tiled=True).reshape(HALF, C1)

time: 73.3 us -> 72.3 us (0.986)
  transfers between devices with their start and end apart: 9 -> 9, of which waited for: 3 -> 4; matrix products, arithmetic and copies ran while one was open for 0% -> 0% of each run, Pallas kernels for 8% -> 8%
where the time goes in v1:
time: 72.3 us; the launch traced here: 72 us
  blocking collectives  32.1 us (44%)
  starting transfers between devices  23.5 us (33%)
  Pallas kernels  9.49 us (13%)
  waiting for transfers between devices  6.01 us (8%)
    all_to_all x1, blocking collectives, backward(): lax.all_to_all(half.reshape(GROUP, CHUNK, C1), group, 0, 0, tiled=True)  17.9 us
    all_to_all x1, blocking collectives, backward(): mine = lax.all_to_all(chunk, group, 0, 0, tiled=True).reshape(HALF, C1)  14.2 us
    ppermute x1, starting transfers between devices, backward(): hy = lax.ppermute(hy, AZ, from_z)  5.58 us
    ppermute x1, starting transfers between devices, backward(): hx = lax.ppermute(hx, AX, from_x)  4.56 us
    ppermute x1, starting transfers between devices, backward(): other = lax.ppermute(mine, 'core', swap)  4.35 us
    ppermute x1, starting transfers between devices, backward(): down = lax.ppermute(chunk, 'zh', [(i ^ 3, i) for i in range(4)])  2.92 us
    ppermute x1, starting transfers between devices, backward(): far = lax.ppermute(chunk, 'zh', [(i ^ 2, i) for i in range(4)])  2.82 us
    ppermute x1, waiting for transfers between devices, backward(): far = lax.ppermute(chunk, 'zh', [(i ^ 2, i) for i in range(4)])  2.72 us
  transfers between devices with their start and end apart: 9, of which 4 were waited for; matrix products, arithmetic and copies ran while one was open for 0% of the time, Pallas kernels for 8%

profile of v1, /device:TPU:1, one launch (start us, length us, event | category | flops | bytes accessed | tf_op | source)
XLA Modules:
  0.0 72.0 jit_solution(4528224632807192538)
XLA Ops:
  0.6 1.1 %shard_map.77 = (bf16[640,128]{1,0:T(8,128)(2,1)S(1)}, bf16[160,128]{1,0:T(8,128)(2,1)S(1)}, bf16[96,128]{1,0:T(8,128)(2,1)S(1)}) custom-call(bf16[1,2,8,64,128]{4,3,2,1,0:T(8,128)(2,1)} %pre_ref.1, bf16[1,1,4,32,128]{4,3,2,1,0:T(8,128)(2,1)} %og_ref.1), custom_call_target="tpu_custom_call" | custom-call | bytes 500000 | tf_op jit(solution)/shard_map/pallas_call | solution.py:307
  1.7 4.6 %collective-permute-start = (bf16[640,128]{1,0:T(8,128)(2,1)S(1)}, bf16[640,128]{1,0:T(8,128)(2,1)S(1)}, u32[]{:S(2)}, u32[]{:S(2)}) collective-permute-start(bf16[640,128]{1,0:T(8,128)(2,1)S(1)} %get-tuple-element.23), channel_id=1, source_target_pairs={{8,0},{16,8},{24,16},{32,24},{40,32},{48,40},{56,48},{0,56},{9,1},... | collective-permute-start | bytes 491528 | tf_op jit(solution)/shard_map/ppermute | solution.py:387
  6.3 5.6 %collective-permute-start.1 = (bf16[160,128]{1,0:T(8,128)(2,1)S(1)}, bf16[160,128]{1,0:T(8,128)(2,1)S(1)}, u32[]{:S(2)}, u32[]{:S(2)}) collective-permute-start(bf16[160,128]{1,0:T(8,128)(2,1)S(1)} %get-tuple-element.24), channel_id=1, source_target_pairs={{1,0},{2,1},{3,2},{4,3},{5,4},{6,5},{7,6},{0,7},{9,8},{10,9},{11,1... | collective-permute-start | bytes 122888 | tf_op jit(solution)/shard_map/ppermute | solution.py:389
  11.8 0.7 collective-permute-start.2
  12.5 2.1 %shard_map.76 = (bf16[3,384,256]{2,1,0:T(8,128)(2,1)S(1)}, bf16[9,256,256]{2,1,0:T(8,128)(2,1)S(1)}, bf16[4,128,1024]{2,1,0:T(8,128)(2,1)S(1)}, bf16[4,256,128]{...) custom-call(bf16[1,4,16,64,128]{4,3,2,1,0:T(8,128)(2,1)} %u_hbm.1, ...), custom_call_target="tpu_custom_call" | custom-call | bytes 6000000 | tf_op jit(solution)/shard_map/pallas_call | solution.py:326
  14.6 0.8 %collective-permute-done.2.hc_ref = bf16[96,128]{1,0:T(8,128)(2,1)S(1)} collective-permute-done((bf16[96,128]{1,0:T(8,128)(2,1)S(1)}, bf16[96,128]{1,0:T(8,128)(2,1)S(1)}, u32[]{:S(2)}, u32[]{:S(2)}) %collective-permute-start.2) | collective-permute-done | bytes 24608 | tf_op jit(solution)/shard_map/ppermute | solution.py:388
  15.4 0.0 collective-permute-done.1.hy_ref
  15.4 0.0 collective-permute-done.hx_ref
  15.4 1.2 %shard_map.78 = (bf16[1728,256]{1,0:T(8,128)(2,1)S(1)}, bf16[1728,128]{1,0:T(8,128)(2,1)S(1)}, bf16[1728,128]{1,0:T(8,128)(2,1)S(1)}) custom-call(bf16[1,2,8,64,128]{4,3,2,1,0:T(8,128)(2,1)S(1)} %get-tuple-element.21.pre_ref, bf16[1,1,4,32,128]{4,3,2,1,0:T(8,128)(2,1)S(1)} %get-tuple-element.22.og_ref, bf16[640,128]{1,0:T(8,128)(2,1)S(1)} %collective-permute-done.hx_ref, ...), custom_call_target="tpu_custom_call" | custom-call | flops 800000000 | bytes 4000000 | tf_op jit(solution)/shard_map/pallas_call | solution.py:340
  16.6 2.4 %collective-permute-start.3 = (bf16[1728,128]{1,0:T(8,128)(2,1)S(1)}, bf16[1728,128]{1,0:T(8,128)(2,1)S(1)}, u32[]{:S(2)}, u32[]{:S(2)}) collective-permute-start(bf16[1728,128]{1,0:T(8,128)(2,1)S(1)} %get-tuple-element.31), channel_id=1, source_target_pairs={{0,64},{64,0},{1,65},{65,1},{2,66},{66,2},{3,67},{67,3},{4,68},{68... | collective-permute-start | bytes 1327112 | tf_op jit(solution)/shard_map/ppermute | solution.py:393
  19.0 0.8 %shard_map.80 = (bf16[864,128]{1,0:T(8,128)(2,1)S(1)}, bf16[864,128]{1,0:T(8,128)(2,1)S(1)}) custom-call(bf16[1728,256]{1,0:T(8,128)(2,1)S(1)} %get-tuple-element.28.a_ref, bf16[4,128,1024]{2,1,0:T(8,128)(2,1)S(1)} %get-tuple-element.32.u1t_ref), custom_call_target="tpu_custom_call" | custom-call | flops 1200000000 | bytes 3000000 | tf_op jit(solution)/shard_map/pallas_call | solution.py:348
  19.9 0.1 collective-permute-start.4
  20.0 1.5 %collective-permute-done.4.got_one = bf16[864,128]{1,0:T(8,128)(2,1)S(1)} collective-permute-done((bf16[864,128]{1,0:T(8,128)(2,1)S(1)}, bf16[864,128]{1,0:T(8,128)(2,1)S(1)}, u32[]{:S(2)}, u32[]{:S(2)}) %collective-permute-start.4) | collective-permute-done | bytes 221216 | tf_op jit(solution)/shard_map/ppermute | solution.py:395
  21.4 0.0 collective-permute-done.3.got_two
  21.4 0.2 shard_map.81
  21.6 17.9 %all_to_all.10 = bf16[32,88,128]{2,1,0:T(8,128)(2,1)S(1)} all-to-all(bf16[32,88,128]{2,1,0:T(8,128)(2,1)S(1)} %bitcast.6), channel_id=1, replica_groups=mesh['xh'=2,'core'=2,'y'=4,'xl'=2,'zh'=4,'zl'=2] {'xh','xl','zl','y'}, dimensions={0} | all-to-all | bytes 1441792 | tf_op jit(solution)/shard_map/all_to_all | solution.py:399
  39.5 0.1 reduce_sum.12
  39.6 2.9 %collective-permute-start.7 = (bf16[88,128]{1,0:T(8,128)(2,1)S(1)}, bf16[88,128]{1,0:T(8,128)(2,1)S(1)}, u32[]{:S(2)}, u32[]{:S(2)}) collective-permute-start(bf16[88,128]{1,0:T(8,128)(2,1)S(1)} %reduce_sum.12), channel_id=1, source_target_pairs={{6,0},{4,2},{2,4},{0,6},{7,1},{5,3},{3,5},{1,7},{14,8},{12,10},{10... | collective-permute-start | bytes 67592 | tf_op jit(solution)/shard_map/ppermute | solution.py:404
  42.5 0.0 collective-permute-start.6
  42.5 2.8 %collective-permute-start.5 = (bf16[88,128]{1,0:T(8,128)(2,1)S(1)}, bf16[88,128]{1,0:T(8,128)(2,1)S(1)}, u32[]{:S(2)}, u32[]{:S(2)}) collective-permute-start(bf16[88,128]{1,0:T(8,128)(2,1)S(1)} %reduce_sum.12), channel_id=1, source_target_pairs={{4,0},{6,2},{0,4},{2,6},{5,1},{7,3},{1,5},{3,7},{12,8},{14,10},{8,... | collective-permute-start | bytes 67592 | tf_op jit(solution)/shard_map/ppermute | solution.py:402
  45.4 0.0 collective-permute-done.7
  45.4 1.0 %collective-permute-done.6 = bf16[88,128]{1,0:T(8,128)(2,1)S(1)} collective-permute-done((bf16[88,128]{1,0:T(8,128)(2,1)S(1)}, bf16[88,128]{1,0:T(8,128)(2,1)S(1)}, u32[]{:S(2)}, u32[]{:S(2)}) %collective-permute-start.6) | collective-permute-done | bytes 22560 | tf_op jit(solution)/shard_map/ppermute | solution.py:403
  46.4 2.7 %collective-permute-done.5 = bf16[88,128]{1,0:T(8,128)(2,1)S(1)} collective-permute-done((bf16[88,128]{1,0:T(8,128)(2,1)S(1)}, bf16[88,128]{1,0:T(8,128)(2,1)S(1)}, u32[]{:S(2)}, u32[]{:S(2)}) %collective-permute-start.5) | collective-permute-done | bytes 22560 | tf_op jit(solution)/shard_map/ppermute | solution.py:402
  49.1 0.1 broadcast_in_dim.2
  49.2 14.2 %all_to_all.11 = bf16[32,88,128]{2,1,0:T(8,128)(2,1)S(1)} all-to-all(bf16[32,88,128]{2,1,0:T(8,128)(2,1)S(1)} %broadcast_in_dim.2), channel_id=1, replica_groups=mesh['xh'=2,'core'=2,'y'=4,'xl'=2,'zh'=4,'zl'=2] {'xh','xl','zl','y'}, dimensions={0} | all-to-all | bytes 1441792 | tf_op jit(solution)/shard_map/all_to_all | solution.py:407
  63.4 4.4 %collective-permute-start.8 = (bf16[2816,128]{1,0:T(8,128)(2,1)S(1)}, bf16[2816,128]{1,0:T(8,128)(2,1)S(1)}, u32[]{:S(2)}, u32[]{:S(2)}) collective-permute-start(bf16[2816,128]{1,0:T(8,128)(2,1)S(1)} %bitcast.4), channel_id=1, source_target_pairs={{0,64},{64,0},{1,65},{65,1},{2,66},{66,2},{3,67},{67,3},{4,68},{68... | collective-permute-start | bytes 2162696 | tf_op jit(solution)/shard_map/ppermute | solution.py:408
  67.8 2.0 %shard_map.79 = bf16[1,4,16,64,128]{4,3,2,1,0:T(8,128)(2,1)} custom-call(bf16[1728,256]{1,0:T(8,128)(2,1)S(1)} %get-tuple-element.28.a_ref, bf16[3,384,256]{2,1,0:T(8,128)(2,1)S(1)} %get-tuple-element.29.r1_ref), custom_call_target="tpu_custom_call" | custom-call | flops 1200000000 | bytes 3000000 | tf_op jit(solution)/shard_map/pallas_call | solution.py:357
  69.7 1.1 %output.2 = (f32[1728,128]{1,0:T(8,128)}, f32[3456,128]{1,0:T(8,128)}) custom-call(bf16[2816,128]{1,0:T(8,128)(2,1)S(1)} %bitcast.5), custom_call_target="tpu_custom_call" | custom-call | bytes 2000000 | tf_op jit(solution)/shard_map/output/pallas_call | solution.py:362
  70.9 0.0 collective-permute-done.8.half_ref
  70.9 1.1 %output.3 = (f32[1728,128]{1,0:T(8,128)}, f32[3456,128]{1,0:T(8,128)}) custom-call(bf16[2816,128]{1,0:T(8,128)(2,1)S(1)} %collective-permute-done.8.half_ref, f32[1728,128]{1,0:T(8,128)} %get-tuple-element.35.refs_0_, f32[3456,128]{1,0:T(8,128)} %get-tuple-element.36.refs_1_), custom_call_target="tpu_custom_call", output_to_operand_aliasing={{0}: (1, {}), {1}: (2, {})} | custom-call | bytes 2000000 | tf_op jit(solution)/shard_map/output/pallas_call | solution.py:362
  (1 shorter events, 0.0 us)
Async XLA Ops:
  1.7 13.7 %collective-permute-start = (bf16[640,128]{1,0:T(8,128)(2,1)S(1)}, bf16[640,128]{1,0:T(8,128)(2,1)S(1)}, u32[]{:S(2)}, u32[]{:S(2)}) collective-permute-start(bf16[640,128]{1,0:T(8,128)(2,1)S(1)} %get-tuple-element.23), channel_id=1, source_target_pairs={{8,0},{16,8},{24,16},{32,24},{40,32},{48,40},{56,48},{0,56},{9,1},... | collective-permute-start | bytes 491528 | tf_op jit(solution)/shard_map/ppermute | solution.py:387
  6.3 9.2 %collective-permute-start.1 = (bf16[160,128]{1,0:T(8,128)(2,1)S(1)}, bf16[160,128]{1,0:T(8,128)(2,1)S(1)}, u32[]{:S(2)}, u32[]{:S(2)}) collective-permute-start(bf16[160,128]{1,0:T(8,128)(2,1)S(1)} %get-tuple-element.24), channel_id=1, source_target_pairs={{1,0},{2,1},{3,2},{4,3},{5,4},{6,5},{7,6},{0,7},{9,8},{10,9},{11,1... | collective-permute-start | bytes 122888 | tf_op jit(solution)/shard_map/ppermute | solution.py:389
  11.8 3.6 %collective-permute-start.2 = (bf16[96,128]{1,0:T(8,128)(2,1)S(1)}, bf16[96,128]{1,0:T(8,128)(2,1)S(1)}, u32[]{:S(2)}, u32[]{:S(2)}) collective-permute-start(bf16[96,128]{1,0:T(8,128)(2,1)S(1)} %get-tuple-element.25), channel_id=1, source_target_pairs={{9,0},{10,1},{11,2},{12,3},{13,4},{14,5},{15,6},{8,7},{17,8},{18,9... | collective-permute-start | bytes 73736 | tf_op jit(solution)/shard_map/ppermute | solution.py:388
  16.6 4.9 %collective-permute-start.3 = (bf16[1728,128]{1,0:T(8,128)(2,1)S(1)}, bf16[1728,128]{1,0:T(8,128)(2,1)S(1)}, u32[]{:S(2)}, u32[]{:S(2)}) collective-permute-start(bf16[1728,128]{1,0:T(8,128)(2,1)S(1)} %get-tuple-element.31), channel_id=1, source_target_pairs={{0,64},{64,0},{1,65},{65,1},{2,66},{66,2},{3,67},{67,3},{4,68},{68... | collective-permute-start | bytes 1327112 | tf_op jit(solution)/shard_map/ppermute | solution.py:393
  19.9 1.6 %collective-permute-start.4 = (bf16[864,128]{1,0:T(8,128)(2,1)S(1)}, bf16[864,128]{1,0:T(8,128)(2,1)S(1)}, u32[]{:S(2)}, u32[]{:S(2)}) collective-permute-start(bf16[864,128]{1,0:T(8,128)(2,1)S(1)} %get-tuple-element.34), channel_id=1, source_target_pairs={{0,64},{64,0},{1,65},{65,1},{2,66},{66,2},{3,67},{67,3},{4,68},{68... | collective-permute-start | bytes 663560 | tf_op jit(solution)/shard_map/ppermute | solution.py:395
  39.6 5.7 %collective-permute-start.7 = (bf16[88,128]{1,0:T(8,128)(2,1)S(1)}, bf16[88,128]{1,0:T(8,128)(2,1)S(1)}, u32[]{:S(2)}, u32[]{:S(2)}) collective-permute-start(bf16[88,128]{1,0:T(8,128)(2,1)S(1)} %reduce_sum.12), channel_id=1, source_target_pairs={{6,0},{4,2},{2,4},{0,6},{7,1},{5,3},{3,5},{1,7},{14,8},{12,10},{10... | collective-permute-start | bytes 67592 | tf_op jit(solution)/shard_map/ppermute | solution.py:404
  42.5 3.8 %collective-permute-start.6 = (bf16[88,128]{1,0:T(8,128)(2,1)S(1)}, bf16[88,128]{1,0:T(8,128)(2,1)S(1)}, u32[]{:S(2)}, u32[]{:S(2)}) collective-permute-start(bf16[88,128]{1,0:T(8,128)(2,1)S(1)} %reduce_sum.12), channel_id=1, source_target_pairs={{2,0},{0,2},{6,4},{4,6},{3,1},{1,3},{7,5},{5,7},{10,8},{8,10},{14,... | collective-permute-start | bytes 67592 | tf_op jit(solution)/shard_map/ppermute | solution.py:403
  42.5 6.6 %collective-permute-start.5 = (bf16[88,128]{1,0:T(8,128)(2,1)S(1)}, bf16[88,128]{1,0:T(8,128)(2,1)S(1)}, u32[]{:S(2)}, u32[]{:S(2)}) collective-permute-start(bf16[88,128]{1,0:T(8,128)(2,1)S(1)} %reduce_sum.12), channel_id=1, source_target_pairs={{4,0},{6,2},{0,4},{2,6},{5,1},{7,3},{1,5},{3,7},{12,8},{14,10},{8,... | collective-permute-start | bytes 67592 | tf_op jit(solution)/shard_map/ppermute | solution.py:402
  63.4 7.4 %collective-permute-start.8 = (bf16[2816,128]{1,0:T(8,128)(2,1)S(1)}, bf16[2816,128]{1,0:T(8,128)(2,1)S(1)}, u32[]{:S(2)}, u32[]{:S(2)}) collective-permute-start(bf16[2816,128]{1,0:T(8,128)(2,1)S(1)} %bitcast.4), channel_id=1, source_target_pairs={{0,64},{64,0},{1,65},{65,1},{2,66},{66,2},{3,67},{67,3},{4,68},{68... | collective-permute-start | bytes 2162696 | tf_op jit(solution)/shard_map/ppermute | solution.py:408
